TPU v7x, 256 devices: a whole 4x4x8 slice. The times are simulated.
256 devices in a mesh: group: 2 (over y_hi), fsdp: 128 (over y_lo, z, x, core).
Axes of the slice: x: 4, y: 4 (y_hi: 2, y_lo: 2; y = y_hi * 2 + y_lo), z: 8, core: 2. Of those that a mesh axis runs over, the one named last changes fastest.
Arguments:
- teacher_rows: bfloat16 [163840, 2048], P(('group', 'fsdp')), may hold values from -6 to 6
- student_rows: bfloat16 [163840, 1024], P(('group', 'fsdp')), may hold values from -24 to 24
- counts: int32 [256], P(('group', 'fsdp')), may hold values from 213 to 640, as said below
- teacher_weight: bfloat16 [2048, 4096], P(None, ('group', 'fsdp')), may hold values from -0.125 to 0.125
- teacher_bias: float32 [4096], replicated, may hold values from -6 to 6
- teacher_gain: float32 [4096], replicated, may hold values from 0.1 to 1.9
- teacher_head: float32 [4096], replicated, may hold values from -0.09375 to 0.09375
- cross_weight: bfloat16 [1024, 1024], replicated, may hold values from -0.1875 to 0.1875
- cross_bias: float32 [1024], replicated, may hold values from -3 to 3
- out_weight: float32 [1024], replicated, may hold values from -0.1875 to 0.1875
Outputs:
- grad_cross: float32 [1024, 1024], P('fsdp')
- grad_bias: float32 [1024], replicated
- grad_out: float32 [1024], replicated
Inputs may be any that keep to these rules, and one draw needn't show every extreme that they name: counts[i] live impressions fill the first slots of shard i, the rest of its 640 slots are padding.
All inputs are finite; a program needn't handle non-finite values.
Results may differ from a plain program's by a relative error of at most 0.00035.
The roundings to bfloat16 on the way count: a program that leaves them out, or rounds other values in their place, can miss the bound.
Values may be sent and summed in bfloat16 or wider, within the bound.
No kernel may reach another device: no remote copies, remote signals or barrier semaphores. Data moves between devices by JAX's collectives and lax.ppermute only.
A program may use at most 128 MiB of HBM per device.

v0:
```python
import math
import jax
import jax.numpy as jnp
from jax import lax
from jax.sharding import Mesh
from jax.sharding import PartitionSpec as P

FSDP = ("fsdp_0", "fsdp_1", "fsdp_2", "fsdp_3")
GROUP_FSDP = ("group", "fsdp_0", "fsdp_1", "fsdp_2", "fsdp_3")
epsilon = 1e-06


def cut_along(shard, dim, count):
    shape = shard.shape
    parts = shard.reshape(*shape[:dim], count, shape[dim] // count, *shape[dim + 1 :])
    return jnp.moveaxis(parts, dim, 0)


def summed_on_arrival(shard, axis, dim):
    count = lax.axis_size(axis)
    parts = lax.all_to_all(cut_along(shard, dim, count), axis, 0, 0, tiled=True)
    return jnp.sum(parts, axis=0)


def sum_by_axis(shard, axes, dim):
    far, near = axes
    parts = cut_along(shard, dim, lax.axis_size(far))
    nearer = summed_on_arrival(parts, near, dim + 1)
    arrived = lax.all_to_all(nearer, far, split_axis=0, concat_axis=0, tiled=True)
    return arrived.sum(axis=0)


def sent_to_all(shard, axis):
    count = lax.axis_size(axis)
    return lax.all_to_all(
        jnp.broadcast_to(shard[None], (count, *shard.shape)), axis, 0, 0, tiled=True
    )


def taken_together(shard, axis):
    return sent_to_all(shard, axis).sum(axis=0)


def over_axes(shard, axes):
    for axis in axes:
        shard = lax.psum(shard, axis)
    return shard


def shards(
    teacher_rows,
    student_rows,
    counts,
    teacher_weight,
    teacher_bias,
    teacher_gain,
    teacher_head,
    cross_weight,
    cross_bias,
    out_weight,
):
    row_count = teacher_rows.shape[0]
    width_s = cross_weight.shape[0]
    group_count = lax.axis_size("group")
    fsdp_count = lax.axis_size(FSDP)
    shard_count = group_count * fsdp_count
    loss_scale = math.sqrt(width_s / (row_count * shard_count))
    preact = jnp.dot(
        teacher_rows,
        lax.all_gather(teacher_weight, GROUP_FSDP, axis=1, tiled=True),
        preferred_element_type=jnp.float32,
    )
    preact = preact + teacher_bias
    meansq = jnp.mean(preact * preact, axis=-1, keepdims=True)
    normed = preact * lax.rsqrt(meansq + epsilon) * teacher_gain
    teacher_logit = jnp.sum(jax.nn.silu(normed) * teacher_head, axis=-1)
    cross = jnp.dot(student_rows, cross_weight, preferred_element_type=jnp.float32) + cross_bias
    inputs_f = student_rows.astype(jnp.float32)
    mixed = inputs_f * cross + inputs_f
    student_logit = jnp.sum(mixed * out_weight, axis=-1)
    live_rows = (jnp.arange(row_count, dtype=jnp.int32) < counts[0]).astype(jnp.float32)
    error = (student_logit - teacher_logit) * live_rows * loss_scale
    dcross = error[:, None] * out_weight[None, :] * inputs_f
    dcross_half = dcross.astype(jnp.bfloat16)
    term_b = jnp.sum(dcross, axis=0)
    term_o = jnp.sum(error[:, None] * mixed, axis=0)
    shard_sum = sum_by_axis(
        lax.dot_general(
            student_rows, dcross_half, (((0,), (0,)), ((), ())), preferred_element_type=jnp.float32
        ),
        (("fsdp_0", "fsdp_1", "fsdp_2"), "fsdp_3"),
        0,
    )
    grad_cross = taken_together(shard_sum, "group")
    small_sums = (over_axes(term_b, GROUP_FSDP), over_axes(term_o, GROUP_FSDP))
    return (grad_cross, small_sums[0], small_sums[1])


def solution(mesh):
    split = Mesh(
        mesh.devices.reshape(mesh.shape["group"], 2, 8, 4, 2),
        ("group", "fsdp_0", "fsdp_1", "fsdp_2", "fsdp_3"),
    )
    in_specs = (
        P(GROUP_FSDP, None),
        P(GROUP_FSDP, None),
        P(GROUP_FSDP),
        P(None, GROUP_FSDP),
        P(),
        P(),
        P(),
        P(),
        P(),
        P(),
    )
    out_specs = (P(FSDP, None), P(), P())
    return jax.shard_map(
        shards, mesh=split, in_specs=in_specs, out_specs=out_specs, check_vma=False
    )
```

profile of v0, /device:TPU:1, one launch (start us, length us, event | category | flops | bytes accessed | tf_op | source)
XLA Modules:
  0.0 295.3 jit_solution(10121287362521425359)
XLA Ops:
  7.2 0.0 copy-start
  7.2 0.0 all-gather.2.cloned.1.call-start
  7.2 0.7 all-gather.2.cloned.1.call-update
  8.6 0.0 copy-start.2
  8.6 5.6 %multiply_reduce_fusion.3 = (f32[640]{0:T(1024)S(1)}, f32[640,1024]{1,0:T(8,128)}) fusion(f32[1024]{0:T(1024)} %param.19, f32[1024]{0:T(1024)} %param.18, bf16[640,1024]{1,0:T(8,128)(2,1)} %param.11, bf16[1024,1024]{1,0:T(8,128)(2,1)} %param.17), kind=kOutput, calls=%fused_computation.8 | convolution fusion | flops 1346108800 | bytes 6040064 | tf_op jit(solution)/shard_map/dot_general | solution.py:77
  14.2 126.8 %all-gather.2.cloned.1.call-done = bf16[2048,4096]{0,1:T(8,128)(2,1)} async-done(((bf16[2048,16]{0,1:T(8,128)(2,1)}), bf16[2048,4096]{0,1:T(8,128)(2,1)}) %all-gather.2.cloned.1.call-update) | async-done | bytes 16777232 | tf_op jit(solution)/shard_map/all_gather | solution.py:70
  141.0 0.0 copy-done
  141.0 0.0 copy-done.2
  141.0 17.0 %multiply_reduce_fusion.1 = (f32[640]{0:T(1024)S(1)}, f32[640,4096]{1,0:T(8,128)}) fusion(f32[4096]{0:T(1024)S(1)} %copy-done.2, bf16[640,2048]{1,0:T(8,128)(2,1)S(1)} %copy-done, bf16[2048,4096]{0,1:T(8,128)(2,1)} %all-gather.2.cloned.1.call-done), kind=kOutput, calls=%fused_computation.1 | convolution fusion | flops 10745281536 | bytes 29903360 | tf_op jit(solution)/shard_map/dot_general | solution.py:68
  158.0 0.0 copy-done.3
  158.0 0.0 copy-done.4
  158.0 0.0 copy-start.1
  158.0 0.0 copy-start.5
  158.0 6.8 %multiply_reduce_fusion = f32[640]{0:T(1024)S(1)} fusion(f32[640,4096]{1,0:T(8,128)} %get-tuple-element.18, f32[4096]{0:T(1024)S(1)} %copy-done.3, f32[4096]{0:T(1024)S(1)} %copy-done.4, f32[640]{0:T(1024)S(1)} %add_rsqrt_fusion, f32[4096]{0:T(1024)S(1)} %copy-done.2), kind=kLoop, calls=%fused_computation | loop fusion | flops 23592320 | bytes 10540032 | tf_op jit(solution)/shard_map/reduce_sum | solution.py:76
  164.8 0.0 copy-done.1
  164.9 0.0 copy-done.5
  164.9 2.0 fusion.2
  166.8 0.6 copy.16
  167.4 8.0 %all_to_all.15 = f32[2,64,8,1024]{3,2,1,0:T(8,128)} all-to-all(f32[2,64,8,1024]{3,2,1,0:T(8,128)S(1)} %bitcast.13), channel_id=1, replica_groups=mesh['group'=2,'fsdp_0'=2,'fsdp_1'=8,'fsdp_2'=4,'fsdp_3'=2] {'fsdp_3'}, dimensions={0} | all-to-all | bytes 8388608 | tf_op jit(solution)/shard_map/all_to_all | solution.py:21
  175.5 4.1 %reduce_sum.75 = f32[64,8,1024]{2,1,0:T(8,128)} reduce(f32[2,64,8,1024]{3,2,1,0:T(8,128)} %all_to_all.15, f32[]{:T(128)} %constant.3.clone.1), dimensions={0}, to_apply=%region_3.4 | reduce | flops 524288 | bytes 6291460 | tf_op jit(solution)/shard_map/reduce_sum | solution.py:22
  179.6 55.6 %all_to_all.16 = f32[64,8,1024]{2,1,0:T(8,128)} all-to-all(f32[64,8,1024]{2,1,0:T(8,128)} %reduce_sum.75), channel_id=1, replica_groups=mesh['group'=2,'fsdp_0'=2,'fsdp_1'=8,'fsdp_2'=4,'fsdp_3'=2] {'fsdp_0','f..., dimensions={0} | all-to-all | bytes 4194304 | tf_op jit(solution)/shard_map/all_to_all | solution.py:29
  235.2 1.7 reduce_sum.76
  237.0 0.6 broadcast_in_dim.2
  237.6 3.3 %all-to-all-start.2 = ((f32[2,8,1024]{2,1,0:T(8,128)}), f32[2,8,1024]{2,1,0:T(8,128)S(1)}, u32[]{:S(2)}, u32[]{:S(2)}) async-start(f32[2,8,1024]{2,1,0:T(8,128)} %broadcast_in_dim.2), calls=%async_computation.2 | async-start | bytes 131072 | tf_op jit(solution)/shard_map/all_to_all | solution.py:35
  240.9 2.7 multiply_reduce_fusion.2
  243.6 5.3 %all-reduce.4 = (f32[1024]{0:T(1024)S(1)}, f32[1024]{0:T(1024)S(1)}) all-reduce(f32[1024]{0:T(1024)S(1)} %get-tuple-element.4, f32[1024]{0:T(1024)S(1)} %get-tuple-element.3), channel_id=1, replica_groups=mesh['group'=2,'fsdp_0'=2,'fsdp_1'=8,'fsdp_2'=4,'fsdp_3'=2] {'group'}, use_global_device_ids=true, to_apply=%region_7.8 | all-reduce | flops 2048 | bytes 16384 | tf_op jit(solution)/shard_map/psum | solution.py:46
  248.9 4.1 %all-reduce.3 = (f32[1024]{0:T(1024)S(1)}, f32[1024]{0:T(1024)S(1)}) all-reduce(f32[1024]{0:T(1024)S(1)} %get-tuple-element.13, f32[1024]{0:T(1024)S(1)} %get-tuple-element.14), channel_id=1, replica_groups=mesh['group'=2,'fsdp_0'=2,'fsdp_1'=8,'fsdp_2'=4,'fsdp_3'=2] {'fsdp_0'}, use_global_device_ids=true, to_apply=%region_8.9 | all-reduce | flops 2048 | bytes 16384 | tf_op jit(solution)/shard_map/psum | solution.py:46
  253.1 14.0 %all-reduce = (f32[1024]{0:T(1024)S(1)}, f32[1024]{0:T(1024)S(1)}) all-reduce(f32[1024]{0:T(1024)S(1)} %get-tuple-element.11, f32[1024]{0:T(1024)S(1)} %get-tuple-element.12), channel_id=1, replica_groups=mesh['group'=2,'fsdp_0'=2,'fsdp_1'=8,'fsdp_2'=4,'fsdp_3'=2] {'fsdp_1'}, use_global_device_ids=true, to_apply=%region_9.10 | all-reduce | flops 2048 | bytes 16384 | tf_op jit(solution)/shard_map/psum | solution.py:46
  267.1 8.2 %all-reduce.1 = (f32[1024]{0:T(1024)S(1)}, f32[1024]{0:T(1024)S(1)}) all-reduce(f32[1024]{0:T(1024)S(1)} %get-tuple-element.5, f32[1024]{0:T(1024)S(1)} %get-tuple-element.6), channel_id=1, replica_groups=mesh['group'=2,'fsdp_0'=2,'fsdp_1'=8,'fsdp_2'=4,'fsdp_3'=2] {'fsdp_2'}, use_global_device_ids=true, to_apply=%region_10.11 | all-reduce | flops 2048 | bytes 16384 | tf_op jit(solution)/shard_map/psum | solution.py:46
  275.3 12.5 %all-reduce.2 = (f32[1024]{0:T(1024)}, f32[1024]{0:T(1024)}) all-reduce(f32[1024]{0:T(1024)S(1)} %get-tuple-element.7, f32[1024]{0:T(1024)S(1)} %get-tuple-element.8), channel_id=1, replica_groups=mesh['group'=2,'fsdp_0'=2,'fsdp_1'=8,'fsdp_2'=4,'fsdp_3'=2] {'fsdp_3'}, use_global_device_ids=true, to_apply=%region_11.12 | all-reduce | flops 2048 | bytes 16384 | tf_op jit(solution)/shard_map/psum | solution.py:46
  287.8 0.0 all-to-all-done.2
  287.8 0.6 reduce_sum.77
  (4 shorter events, 0.0 us)
Async XLA Ops:
  7.2 133.8 %copy-start = (bf16[640,2048]{1,0:T(8,128)(2,1)S(1)}, bf16[640,2048]{1,0:T(8,128)(2,1)}, u32[]{:S(2)}) copy-start(bf16[640,2048]{1,0:T(8,128)(2,1)} %param.10) | copy-start | bytes 7864324
  7.2 133.8 %all-gather.2.cloned.1.call-start = ((), (), s32[]{:S(2)}) async-start(), calls=%async_computation.3 | async-start | bytes 16842752 | tf_op jit(solution)/shard_map/all_gather | solution.py:70
  8.6 132.4 %copy-start.2 = (f32[4096]{0:T(1024)S(1)}, f32[4096]{0:T(1024)}, u32[]{:S(2)}) copy-start(f32[4096]{0:T(1024)} %param.14) | copy-start | bytes 49156
  14.2 143.8 %copy-start.3 = (f32[4096]{0:T(1024)S(1)}, f32[4096]{0:T(1024)}, u32[]{:S(2)}) copy-start(f32[4096]{0:T(1024)} %param.16) | copy-start | bytes 49156
  14.2 143.8 %copy-start.4 = (f32[4096]{0:T(1024)S(1)}, f32[4096]{0:T(1024)}, u32[]{:S(2)}) copy-start(f32[4096]{0:T(1024)} %param.15) | copy-start | bytes 49156
  158.0 6.8 %copy-start.1 = (bf16[640,1024]{1,0:T(8,128)(2,1)S(1)}, bf16[640,1024]{1,0:T(8,128)(2,1)}, u32[]{:S(2)}) copy-start(bf16[640,1024]{1,0:T(8,128)(2,1)} %param.11) | copy-start | bytes 3932164
  158.0 6.8 %copy-start.5 = (f32[1024]{0:T(1024)S(1)}, f32[1024]{0:T(1024)}, u32[]{:S(2)}) copy-start(f32[1024]{0:T(1024)} %param.19) | copy-start | bytes 12292
  237.6 50.2 %all-to-all-start.2 = ((f32[2,8,1024]{2,1,0:T(8,128)}), f32[2,8,1024]{2,1,0:T(8,128)S(1)}, u32[]{:S(2)}, u32[]{:S(2)}) async-start(f32[2,8,1024]{2,1,0:T(8,128)} %broadcast_in_dim.2), calls=%async_computation.2 | async-start | bytes 131072 | tf_op jit(solution)/shard_map/all_to_all | solution.py:35
Sparse Core Ops, SparseCore 0:
  11.6 129.3 all-gather.1
where the time goes:
time: 296 us; the launch traced here: 295 us
  waiting for transfers between devices  127 us (43%)
  blocking collectives  108 us (36%)
  matrix products  24.6 us (8%)
  other arithmetic  16 us (5%)
  between operations  14.9 us (5%)
  starting transfers between devices  3.33 us (1%)
    all_gather x1, waiting for transfers between devices, shards(): lax.all_gather(teacher_weight, GROUP_FSDP, axis=1, tiled=True)  127 us
    all_to_all x1, blocking collectives, sum_by_axis(): lax.all_to_all(nearer, far, split_axis=0, concat_axis=0, tiled=True)  55.6 us
    psum x5, blocking collectives, over_axes(): shard = lax.psum(shard, axis)  44.2 us
    dot_general x1, matrix products, shards(): jnp.dot(teacher_rows, lax.all_gather(teacher_weight, GROUP_FSDP, axis=1,...  17 us
    all_to_all x1, blocking collectives, summed_on_arrival(): parts = lax.all_to_all(cut_along(shard, dim, count), axis, 0, 0, tiled=True)  8.05 us
    reduce_sum x1, other arithmetic, shards(): teacher_logit = jnp.sum(jax.nn.silu(normed) * teacher_head, axis=-1)  6.78 us
  transfers between devices with their start and end apart: 2, of which 1 were waited for; matrix products, arithmetic and copies ran while one was open for 3% of the time, Pallas kernels for 0%

commit v1 on v0

--- a/solution.py
+++ b/solution.py
@@ -43,7 +43,7 @@
 
 def over_axes(shard, axes):
     for axis in axes:
-        shard = lax.psum(shard, axis)
+        shard = jnp.sum(lax.all_gather(shard, axis), axis=0)
     return shard
 
 

time: 296 us -> 333 us (1.12)
  blocking collectives: 108 us -> 135 us
  starting transfers between devices: 3.33 us -> 11.1 us
    all_gather x0 -> x10, blocking collectives: none -> 127 us  [over_axes(): shard = jnp.sum(lax.all_gather(shard, axis), axis=0)]
    all_to_all x1 -> x0, blocking collectives: 55.6 us -> none  [sum_by_axis(): lax.all_to_all(nearer, far, split_axis=0, concat_axis=0, tiled=True)]
    psum x5 -> x0, blocking collectives: 44.2 us -> none  [over_axes(): shard = lax.psum(shard, axis)]
    all_to_all x0 -> x1, starting transfers between devices: none -> 7.76 us  [sum_by_axis(): lax.all_to_all(nearer, far, split_axis=0, concat_axis=0, tiled=True)]
  transfers between devices with their start and end apart: 2 -> 3, of which waited for: 1 -> 1; matrix products, arithmetic and copies ran while one was open for 3% -> 3% of each run, Pallas kernels for 0% -> 0%
where the time goes in v1:
time: 333 us; the launch traced here: 332 us
  blocking collectives  135 us (41%)
  waiting for transfers between devices  127 us (38%)
  matrix products  24.6 us (7%)
  other arithmetic  17.3 us (5%)
  between operations  14.9 us (4%)
  starting transfers between devices  11.1 us (3%)
    all_gather x10, blocking collectives, over_axes(): shard = jnp.sum(lax.all_gather(shard, axis), axis=0)  127 us
    all_gather x1, waiting for transfers between devices, shards(): lax.all_gather(teacher_weight, GROUP_FSDP, axis=1, tiled=True)  127 us
    dot_general x1, matrix products, shards(): jnp.dot(teacher_rows, lax.all_gather(teacher_weight, GROUP_FSDP, axis=1,...  17 us
    all_to_all x1, blocking collectives, summed_on_arrival(): parts = lax.all_to_all(cut_along(shard, dim, count), axis, 0, 0, tiled=True)  8.05 us
    all_to_all x1, starting transfers between devices, sum_by_axis(): lax.all_to_all(nearer, far, split_axis=0, concat_axis=0, tiled=True)  7.76 us
    reduce_sum x1, other arithmetic, shards(): teacher_logit = jnp.sum(jax.nn.silu(normed) * teacher_head, axis=-1)  6.78 us
  transfers between devices with their start and end apart: 3, of which 1 were waited for; matrix products, arithmetic and copies ran while one was open for 3% of the time, Pallas kernels for 0%

profile of v1, /device:TPU:1, one launch (start us, length us, event | category | flops | bytes accessed | tf_op | source)
XLA Modules:
  0.0 331.7 jit_solution(901030935351622454)
XLA Ops:
  7.2 0.0 copy-start
  7.2 0.0 all-gather.12.cloned.1.call-start
  7.2 0.7 all-gather.12.cloned.1.call-update
  8.6 5.6 %multiply_reduce_fusion.3 = (f32[640]{0:T(1024)S(1)}, f32[640,1024]{1,0:T(8,128)}) fusion(f32[1024]{0:T(1024)} %param.19, f32[1024]{0:T(1024)} %param.18, bf16[640,1024]{1,0:T(8,128)(2,1)} %param.11, bf16[1024,1024]{1,0:T(8,128)(2,1)} %param.17), kind=kOutput, calls=%fused_computation.8 | convolution fusion | flops 1346108800 | bytes 6040064 | tf_op jit(solution)/shard_map/dot_general | solution.py:77
  14.2 126.8 %all-gather.12.cloned.1.call-done = bf16[2048,4096]{0,1:T(8,128)(2,1)} async-done(((bf16[2048,16]{0,1:T(8,128)(2,1)}), bf16[2048,4096]{0,1:T(8,128)(2,1)}) %all-gather.12.cloned.1.call-update) | async-done | bytes 16777232 | tf_op jit(solution)/shard_map/all_gather | solution.py:70
  141.0 17.0 %multiply_reduce_fusion.1 = (f32[640]{0:T(1024)S(1)}, f32[640,4096]{1,0:T(8,128)}) fusion(f32[4096]{0:T(1024)S(1)} %copy-done.2, bf16[640,2048]{1,0:T(8,128)(2,1)S(1)} %copy-done, bf16[2048,4096]{0,1:T(8,128)(2,1)} %all-gather.12.cloned.1.call-done), kind=kOutput, calls=%fused_computation.1 | convolution fusion | flops 10745281536 | bytes 29903360 | tf_op jit(solution)/shard_map/dot_general | solution.py:68
  158.0 0.0 copy-start.1
  158.0 0.0 copy-start.5
  158.0 6.8 %multiply_reduce_fusion = f32[640]{0:T(1024)S(1)} fusion(f32[640,4096]{1,0:T(8,128)} %get-tuple-element.8, f32[4096]{0:T(1024)S(1)} %copy-done.3, f32[4096]{0:T(1024)S(1)} %copy-done.4, f32[640]{0:T(1024)S(1)} %add_rsqrt_fusion, f32[4096]{0:T(1024)S(1)} %copy-done.2), kind=kLoop, calls=%fused_computation | loop fusion | flops 23592320 | bytes 10540032 | tf_op jit(solution)/shard_map/reduce_sum | solution.py:76
  164.9 2.0 fusion.2
  166.8 0.6 copy.16
  167.4 8.0 %all_to_all.15 = f32[2,64,8,1024]{3,2,1,0:T(8,128)} all-to-all(f32[2,64,8,1024]{3,2,1,0:T(8,128)S(1)} %bitcast.13), channel_id=1, replica_groups=mesh['group'=2,'fsdp_0'=2,'fsdp_1'=8,'fsdp_2'=4,'fsdp_3'=2] {'fsdp_3'}, dimensions={0} | all-to-all | bytes 8388608 | tf_op jit(solution)/shard_map/all_to_all | solution.py:21
  175.5 4.1 %reduce_sum.165 = f32[64,8,1024]{2,1,0:T(8,128)} reduce(f32[2,64,8,1024]{3,2,1,0:T(8,128)} %all_to_all.15, f32[]{:T(128)} %constant.3.clone.1), dimensions={0}, to_apply=%region_3.4 | reduce | flops 524288 | bytes 6291460 | tf_op jit(solution)/shard_map/reduce_sum | solution.py:22
  179.6 7.8 %all-to-all-start.1 = ((f32[64,8,1024]{2,1,0:T(8,128)}), f32[64,8,1024]{2,1,0:T(8,128)}, u32[]{:S(2)}, u32[]{:S(2)}) async-start(f32[64,8,1024]{2,1,0:T(8,128)} %reduce_sum.165), calls=%async_computation.1 | async-start | bytes 4194304 | tf_op jit(solution)/shard_map/all_to_all | solution.py:29
  187.4 2.7 multiply_reduce_fusion.2
  190.1 5.4 %all-gather = f32[2048]{0:T(1024)S(1)} all-gather(f32[1024]{0:T(1024)S(1)} %get-tuple-element.4), channel_id=2, replica_groups=mesh['group'=2,'fsdp_0'=2,'fsdp_1'=8,'fsdp_2'=4,'fsdp_3'=2] {'group'}, dimensions={0}, use_global_device_ids=true | all-gather | bytes 12288 | tf_op jit(solution)/shard_map/all_gather | solution.py:46
  195.5 3.6 %all-gather.1 = f32[2048]{0:T(1024)S(1)} all-gather(f32[1024]{0:T(1024)S(1)} %reduce_sum.169), channel_id=3, replica_groups=mesh['group'=2,'fsdp_0'=2,'fsdp_1'=8,'fsdp_2'=4,'fsdp_3'=2] {'fsdp_0'}, dimensions={0}, use_global_device_ids=true | all-gather | bytes 12288 | tf_op jit(solution)/shard_map/all_gather | solution.py:46
  199.1 49.1 %all-gather.2 = f32[8192]{0:T(1024)S(1)} all-gather(f32[1024]{0:T(1024)S(1)} %reduce_sum.170), channel_id=4, replica_groups=mesh['group'=2,'fsdp_0'=2,'fsdp_1'=8,'fsdp_2'=4,'fsdp_3'=2] {'fsdp_1'}, dimensions={0}, use_global_device_ids=true | all-gather | bytes 36864 | tf_op jit(solution)/shard_map/all_gather | solution.py:46
  248.3 0.0 all-to-all-done.1
  248.3 1.7 reduce_sum.166
  250.0 0.6 broadcast_in_dim.2
  250.6 3.3 all-to-all-start.2
  253.9 9.6 %all-gather.3 = f32[4096]{0:T(1024)S(1)} all-gather(f32[1024]{0:T(1024)S(1)} %reduce_sum.171), channel_id=5, replica_groups=mesh['group'=2,'fsdp_0'=2,'fsdp_1'=8,'fsdp_2'=4,'fsdp_3'=2] {'fsdp_2'}, dimensions={0}, use_global_device_ids=true | all-gather | bytes 20480 | tf_op jit(solution)/shard_map/all_gather | solution.py:46
  263.6 10.5 %all-gather.4 = f32[2048]{0:T(1024)S(1)} all-gather(f32[1024]{0:T(1024)S(1)} %reduce_sum.172), channel_id=6, replica_groups=mesh['group'=2,'fsdp_0'=2,'fsdp_1'=8,'fsdp_2'=4,'fsdp_3'=2] {'fsdp_3'}, dimensions={0}, use_global_device_ids=true | all-gather | bytes 12288 | tf_op jit(solution)/shard_map/all_gather | solution.py:46
  274.2 0.6 reduce_sum.173
  274.8 5.0 %all-gather.5 = f32[2048]{0:T(1024)S(1)} all-gather(f32[1024]{0:T(1024)S(1)} %get-tuple-element.3), channel_id=7, replica_groups=mesh['group'=2,'fsdp_0'=2,'fsdp_1'=8,'fsdp_2'=4,'fsdp_3'=2] {'group'}, dimensions={0}, use_global_device_ids=true | all-gather | bytes 12288 | tf_op jit(solution)/shard_map/all_gather | solution.py:46
  279.8 3.2 all-gather.6
  283.0 18.3 %all-gather.7 = f32[8192]{0:T(1024)S(1)} all-gather(f32[1024]{0:T(1024)S(1)} %reduce_sum.176), channel_id=9, replica_groups=mesh['group'=2,'fsdp_0'=2,'fsdp_1'=8,'fsdp_2'=4,'fsdp_3'=2] {'fsdp_1'}, dimensions={0}, use_global_device_ids=true | all-gather | bytes 36864 | tf_op jit(solution)/shard_map/all_gather | solution.py:46
  301.4 9.1 %all-gather.8 = f32[4096]{0:T(1024)S(1)} all-gather(f32[1024]{0:T(1024)S(1)} %reduce_sum.177), channel_id=10, replica_groups=mesh['group'=2,'fsdp_0'=2,'fsdp_1'=8,'fsdp_2'=4,'fsdp_3'=2] {'fsdp_2'}, dimensions={0}, use_global_device_ids=true | all-gather | bytes 20480 | tf_op jit(solution)/shard_map/all_gather | solution.py:46
  310.5 13.1 %all-gather.9 = f32[2048]{0:T(1024)S(1)} all-gather(f32[1024]{0:T(1024)S(1)} %reduce_sum.178), channel_id=11, replica_groups=mesh['group'=2,'fsdp_0'=2,'fsdp_1'=8,'fsdp_2'=4,'fsdp_3'=2] {'fsdp_3'}, dimensions={0}, use_global_device_ids=true | all-gather | bytes 12288 | tf_op jit(solution)/shard_map/all_gather | solution.py:46
  323.6 0.6 reduce_sum.179
  324.3 0.6 reduce_sum.167
  (30 shorter events, 0.3 us)
Async XLA Ops:
  7.2 133.8 %copy-start = (bf16[640,2048]{1,0:T(8,128)(2,1)S(1)}, bf16[640,2048]{1,0:T(8,128)(2,1)}, u32[]{:S(2)}) copy-start(bf16[640,2048]{1,0:T(8,128)(2,1)} %param.10) | copy-start | bytes 7864324
  7.2 133.8 %all-gather.12.cloned.1.call-start = ((), (), s32[]{:S(2)}) async-start(), calls=%async_computation.3 | async-start | bytes 16842752 | tf_op jit(solution)/shard_map/all_gather | solution.py:70
  8.6 132.4 %copy-start.2 = (f32[4096]{0:T(1024)S(1)}, f32[4096]{0:T(1024)}, u32[]{:S(2)}) copy-start(f32[4096]{0:T(1024)} %param.14) | copy-start | bytes 49156
  14.2 143.8 %copy-start.3 = (f32[4096]{0:T(1024)S(1)}, f32[4096]{0:T(1024)}, u32[]{:S(2)}) copy-start(f32[4096]{0:T(1024)} %param.16) | copy-start | bytes 49156
  14.2 143.8 %copy-start.4 = (f32[4096]{0:T(1024)S(1)}, f32[4096]{0:T(1024)}, u32[]{:S(2)}) copy-start(f32[4096]{0:T(1024)} %param.15) | copy-start | bytes 49156
  158.0 6.8 %copy-start.1 = (bf16[640,1024]{1,0:T(8,128)(2,1)S(1)}, bf16[640,1024]{1,0:T(8,128)(2,1)}, u32[]{:S(2)}) copy-start(bf16[640,1024]{1,0:T(8,128)(2,1)} %param.11) | copy-start | bytes 3932164
  158.0 6.8 %copy-start.5 = (f32[1024]{0:T(1024)S(1)}, f32[1024]{0:T(1024)}, u32[]{:S(2)}) copy-start(f32[1024]{0:T(1024)} %param.19) | copy-start | bytes 12292
  179.6 68.7 %all-to-all-start.1 = ((f32[64,8,1024]{2,1,0:T(8,128)}), f32[64,8,1024]{2,1,0:T(8,128)}, u32[]{:S(2)}, u32[]{:S(2)}) async-start(f32[64,8,1024]{2,1,0:T(8,128)} %reduce_sum.165), calls=%async_computation.1 | async-start | bytes 4194304 | tf_op jit(solution)/shard_map/all_to_all | solution.py:29
  250.6 73.6 %all-to-all-start.2 = ((f32[2,8,1024]{2,1,0:T(8,128)}), f32[2,8,1024]{2,1,0:T(8,128)S(1)}, u32[]{:S(2)}, u32[]{:S(2)}) async-start(f32[2,8,1024]{2,1,0:T(8,128)} %broadcast_in_dim.2), calls=%async_computation.2 | async-start | bytes 131072 | tf_op jit(solution)/shard_map/all_to_all | solution.py:35
Sparse Core Ops, SparseCore 0:
  11.6 129.3 all-gather.11
